TPU v7x, 256 devices: a whole 4x4x8 slice. The times are simulated.
256 devices in a mesh: dp: 32 (over x, y, core), etp: 8 (over z).
Axes of the slice: x: 4, y: 4, z: 8, core: 2. Of those that a mesh axis runs over, the one named last changes fastest.
Arguments:
- tokens: bfloat16 [8192, 3072], P('dp'), may hold values from -6 to 6
- cotangent: bfloat16 [8192, 3072], P('dp'), may hold values from -6 to 6
- w_gate: float32 [2, 3072, 6144], P(None, 'dp', 'etp'), may hold values from -0.109375 to 0.109375
- w_up: float32 [2, 3072, 6144], P(None, 'dp', 'etp'), may hold values from -0.109375 to 0.109375
- w_down: float32 [2, 6144, 3072], P(None, 'etp', 'dp'), may hold values from -0.078125 to 0.078125
- slot_token: int32 [16384], P('dp'), may hold values from 0 to 255, as said below
- slot_gate: int32 [16384], P('dp'), may hold values from 0 to 16
- block_expert: int32 [128], P('dp'), may hold values from 0 to 2, as said below
Outputs:
- combined: bfloat16 [8192, 3072], P('dp', 'etp')
- input_grad: bfloat16 [8192, 3072], P('dp', 'etp')
Inputs may be any that keep to these rules, and one draw needn't show every extreme that they name: `slot_token`: within the live blocks of one expert on one dp index no token repeats, so each expert has at most 2 live blocks there. `block_expert`: blocks of the experts and padding blocks stand in any order; each expert has at most 2 blocks on one dp index, and on some dp index every block is live.
All inputs are finite; a program needn't handle non-finite values.
Results may differ from a plain program's by a relative error of at most 0.014.
Values may be sent and summed in bfloat16 or wider, within the bound.
A program may use at most 128 MiB of HBM per device.

v0:
```python
import jax
import jax.numpy as jnp
from jax import lax
from jax.sharding import PartitionSpec as P

gate_steps = 16.0


def block_terms(
    gate_mat,
    up_mat,
    down_mat,
    tokens,
    cotangent,
    slot_token,
    scale,
    block_index,
    block_rows,
    totals,
):
    y_total, dx_total = totals
    row_start = block_index * block_rows
    token_rows = lax.dynamic_slice_in_dim(slot_token, row_start, block_rows, 0)
    gate_scale = lax.dynamic_slice_in_dim(scale, row_start, block_rows, 0)[:, None]
    inputs = tokens[token_rows]
    upstream = cotangent[token_rows]
    gate_pre = jnp.dot(inputs, gate_mat, preferred_element_type=jnp.float32)
    up_pre = jnp.dot(inputs, up_mat, preferred_element_type=jnp.float32)
    squash = jax.nn.sigmoid(gate_pre)
    active = gate_pre * squash
    hidden = (active * up_pre).astype(jnp.bfloat16)
    produced = jnp.dot(hidden, down_mat, preferred_element_type=jnp.float32) * gate_scale
    d_out = (gate_scale * upstream.astype(jnp.float32)).astype(jnp.bfloat16)
    contract_last = (((1,), (1,)), ((), ()))
    d_hidden = lax.dot_general(d_out, down_mat, contract_last, preferred_element_type=jnp.float32)
    d_pre = (d_hidden * up_pre * squash * (1.0 + gate_pre * (1.0 - squash))).astype(jnp.bfloat16)
    d_up = (d_hidden * active).astype(jnp.bfloat16)
    backward = lax.dot_general(d_pre, gate_mat, contract_last, preferred_element_type=jnp.float32)
    backward = backward + lax.dot_general(
        d_up, up_mat, contract_last, preferred_element_type=jnp.float32
    )
    return (y_total.at[token_rows].add(produced), dx_total.at[token_rows].add(backward))


def shards(tokens, cotangent, w_gate, w_up, w_down, slot_token, slot_gate, block_expert):
    experts_count = w_gate.shape[0]
    block_count = block_expert.shape[0]
    block_rows = slot_token.shape[0] // block_count
    scale = slot_gate.astype(jnp.float32) / gate_steps
    gate_low = w_gate.astype(jnp.bfloat16)
    up_low = w_up.astype(jnp.bfloat16)
    down_low = w_down.astype(jnp.bfloat16)
    zeroed = jnp.zeros(tokens.shape, jnp.float32)
    totals = (zeroed, zeroed)

    def skip_block(state):
        return state

    gate_all, up_all = (
        lax.all_gather(gate_low, "dp", axis=1, tiled=True),
        lax.all_gather(up_low, "dp", axis=1, tiled=True),
    )
    down_all = lax.all_gather(down_low, "dp", axis=2, tiled=True)

    def visit_all(block_index, state):
        expert = block_expert[block_index]
        chosen = jnp.minimum(expert, experts_count - 1)

        def compute_block(inner):
            gate_mat = lax.dynamic_index_in_dim(gate_all, chosen, 0, keepdims=False)
            up_mat = lax.dynamic_index_in_dim(up_all, chosen, 0, keepdims=False)
            down_mat = lax.dynamic_index_in_dim(down_all, chosen, 0, keepdims=False)
            return block_terms(
                gate_mat,
                up_mat,
                down_mat,
                tokens,
                cotangent,
                slot_token,
                scale,
                block_index,
                block_rows,
                inner,
            )

        return lax.cond(expert < experts_count, compute_block, skip_block, state)

    totals = lax.fori_loop(0, block_count, visit_all, totals)
    combined, input_grad = (
        lax.psum_scatter(
            totals[0].astype(jnp.bfloat16), "etp", scatter_dimension=1, tiled=True
        ).astype(jnp.float32),
        lax.psum_scatter(
            totals[1].astype(jnp.bfloat16), "etp", scatter_dimension=1, tiled=True
        ).astype(jnp.float32),
    )
    return (combined.astype(jnp.bfloat16), input_grad.astype(jnp.bfloat16))


def solution(mesh):
    in_specs = (
        P("dp", None),
        P("dp", None),
        P(None, "dp", "etp"),
        P(None, "dp", "etp"),
        P(None, "etp", "dp"),
        P("dp"),
        P("dp"),
        P("dp"),
    )
    out_specs = (P("dp", "etp"), P("dp", "etp"))
    return jax.shard_map(shards, mesh=mesh, in_specs=in_specs, out_specs=out_specs, check_vma=False)
```

profile of v0, /device:TPU:2, one launch (start us, length us, event | category | flops | bytes accessed | tf_op | source)
XLA Modules:
  0.0 489.7 jit_solution(1903295765239692804)
XLA Ops:
  13.3 60.4 %all-gather.8.cloned.1.call-done = bf16[2,768,3072]{1,0,2:T(2,128)(2,1)} async-done(((bf16[2,768,96]{1,0,2:T(2,128)(2,1)}), bf16[2,768,3072]{1,0,2:T(2,128)(2,1)}) %all-gather.8.cloned.1.call-update) | async-done | bytes 9437200 | tf_op jit(solution)/shard_map/all_gather | solution.py:63
  73.7 23.8 %copy.12 = bf16[2,768,3072]{2,1,0:T(8,128)(2,1)} copy(bf16[2,768,3072]{1,0,2:T(2,128)(2,1)} %all-gather.8.cloned.1.call-done) | data formatting | bytes 18874368 | tf_op jit(solution)/shard_map/while | solution.py:88
  97.5 38.7 %all-gather.4.cloned.1.call-done = bf16[2,3072,768]{2,1,0:T(8,128)(2,1)} async-done(((bf16[2,96,768]{2,1,0:T(8,128)(2,1)}), bf16[2,3072,768]{2,1,0:T(8,128)(2,1)}) %all-gather.4.cloned.1.call-update) | async-done | bytes 9437200 | tf_op jit(solution)/shard_map/all_gather | solution.py:60
  136.2 62.5 %all-gather.6.cloned.1.call-done = bf16[2,3072,768]{2,1,0:T(8,128)(2,1)} async-done(((bf16[2,96,768]{2,1,0:T(8,128)(2,1)}), bf16[2,3072,768]{2,1,0:T(8,128)(2,1)}) %all-gather.6.cloned.1.call-update) | async-done | bytes 9437200 | tf_op jit(solution)/shard_map/all_gather | solution.py:61
  201.1 194.1 %while.15 = (s32[]{:T(128)}, f32[256,3072]{1,0:T(8,128)S(1)}, f32[256,3072]{1,0:T(8,128)}, s32[4]{0:T(128)S(1)}, s32[512]{0:T(512)}, /*index=5*/bf16[256,3072]{1...) while((s32[]{:T(128)}, f32[256,3072]{1,0:T(8,128)S(1)}, ...), condition=%wide.region_5.6_spmd, body=%wide.region_0.5_spmd.sunk | while | flops 3628795392 | bytes 59779048 | solution.py:88
  202.4 47.3 %conditional.2 = ((f32[256,3072]{1,0:T(8,128)S(1)}, f32[256,3072]{1,0:T(8,128)})) conditional(s32[]{:T(128)} %convert_element_type.63, (f32[256,3072]{1,0:T(8,128)S(1)}, f32[256,3072]{1,0:T(8,128)}) %tuple.42, (s32[]{:T(128)}, s32[512]{0:T(512)}, bf16[256,3072]{1,0:T(8,128)(2,1)}, s32[]{:T(128)}, bf16[2,3072,768]{2,1,0:T(8,128)(2,1)}, ...), branch_computations={%region_1.0_spmd, %region_2.4_spmd} | conditional | flops 3628795392 | bytes 59778792 | solution.py:86
  203.8 4.3 gather_fusion.1
  208.2 5.0 %fusion = f32[128,768]{1,0:T(8,128)} fusion(bf16[2,768,3072]{2,1,0:T(8,128)(2,1)} %get-tuple-element.210, s32[]{:T(128)S(6)} %select_n.21, bf16[128,3072]{1,0:T(8,128)(2,1)} %gather_fusion.1, f32[128]{0:T(128)S(1)} %dynamic_slice.22), kind=kOutput, calls=%fused_computation.4 | convolution fusion | flops 605159424 | bytes 5898756 | tf_op jit(solution)/shard_map/while/body/eval_jaxpr/cond/branch_1_fun/dot_general | solution.py:35
  213.3 4.3 gather_fusion
  217.6 3.4 fusion.10
  221.0 4.1 fusion.4
  228.2 5.3 %fusion.18 = f32[128,3072]{1,0:T(8,128)} fusion(f32[128,3072]{1,0:T(8,128)S(1)} %fusion.4, bf16[2,3072,768]{2,1,0:T(8,128)(2,1)} %get-tuple-element.207, s32[]{:T(128)S(6)} %select_n.21, f32[128,768]{1,0:T(8,128)S(1)} %fusion.10, f32[128,768]{1,0:T(8,128)S(1)} %copy-done.2, f32[128,768]{1,0:T(8,128)S(1)} %fusion.6), kind=kOutput, calls=%fused_computation.22 | convolution fusion | flops 605356032 | bytes 9043972 | tf_op jit(solution)/shard_map/while/body/eval_jaxpr/cond/branch_1_fun/dot_general | solution.py:38
  233.5 7.0 %scatter_fusion.1 = f32[256,3072]{1,0:T(8,128)} fusion(f32[256,3072]{1,0:T(8,128)} %get-tuple-element.212, s32[128]{0:T(128)S(1)} %compare_select_fusion, f32[128,3072]{1,0:T(8,128)} %fusion.18), kind=kCustom, calls=%fused_computation.3 | custom fusion | flops 393216 | bytes 4719104 | tf_op jit(solution)/shard_map/while/body/eval_jaxpr/cond/branch_1_fun/scatter-add | solution.py:42
  240.6 4.4 fusion.21
  245.0 4.6 scatter_fusion
  250.9 47.3 %conditional.2 = ((f32[256,3072]{1,0:T(8,128)S(1)}, f32[256,3072]{1,0:T(8,128)})) conditional(s32[]{:T(128)} %convert_element_type.63, (f32[256,3072]{1,0:T(8,128)S(1)}, f32[256,3072]{1,0:T(8,128)}) %tuple.42, (s32[]{:T(128)}, s32[512]{0:T(512)}, bf16[256,3072]{1,0:T(8,128)(2,1)}, s32[]{:T(128)}, bf16[2,3072,768]{2,1,0:T(8,128)(2,1)}, ...), branch_computations={%region_1.0_spmd, %region_2.4_spmd} | conditional | flops 3628795392 | bytes 59778792 | solution.py:86
  252.4 4.3 gather_fusion.1
  256.8 5.0 %fusion = f32[128,768]{1,0:T(8,128)} fusion(bf16[2,768,3072]{2,1,0:T(8,128)(2,1)} %get-tuple-element.210, s32[]{:T(128)S(6)} %select_n.21, bf16[128,3072]{1,0:T(8,128)(2,1)} %gather_fusion.1, f32[128]{0:T(128)S(1)} %dynamic_slice.22), kind=kOutput, calls=%fused_computation.4 | convolution fusion | flops 605159424 | bytes 5898756 | tf_op jit(solution)/shard_map/while/body/eval_jaxpr/cond/branch_1_fun/dot_general | solution.py:35
  261.8 4.3 gather_fusion
  266.2 3.4 fusion.10
  269.6 4.0 fusion.4
  273.6 3.1 fusion.6
  276.8 5.3 %fusion.18 = f32[128,3072]{1,0:T(8,128)} fusion(f32[128,3072]{1,0:T(8,128)S(1)} %fusion.4, bf16[2,3072,768]{2,1,0:T(8,128)(2,1)} %get-tuple-element.207, s32[]{:T(128)S(6)} %select_n.21, f32[128,768]{1,0:T(8,128)S(1)} %fusion.10, f32[128,768]{1,0:T(8,128)S(1)} %copy-done.2, f32[128,768]{1,0:T(8,128)S(1)} %fusion.6), kind=kOutput, calls=%fused_computation.22 | convolution fusion | flops 605356032 | bytes 9043972 | tf_op jit(solution)/shard_map/while/body/eval_jaxpr/cond/branch_1_fun/dot_general | solution.py:38
  282.1 7.0 %scatter_fusion.1 = f32[256,3072]{1,0:T(8,128)} fusion(f32[256,3072]{1,0:T(8,128)} %get-tuple-element.212, s32[128]{0:T(128)S(1)} %compare_select_fusion, f32[128,3072]{1,0:T(8,128)} %fusion.18), kind=kCustom, calls=%fused_computation.3 | custom fusion | flops 393216 | bytes 4719104 | tf_op jit(solution)/shard_map/while/body/eval_jaxpr/cond/branch_1_fun/scatter-add | solution.py:42
  289.1 4.4 fusion.21
  293.6 4.6 scatter_fusion
  299.5 47.3 %conditional.2 = ((f32[256,3072]{1,0:T(8,128)S(1)}, f32[256,3072]{1,0:T(8,128)})) conditional(s32[]{:T(128)} %convert_element_type.63, (f32[256,3072]{1,0:T(8,128)S(1)}, f32[256,3072]{1,0:T(8,128)}) %tuple.42, (s32[]{:T(128)}, s32[512]{0:T(512)}, bf16[256,3072]{1,0:T(8,128)(2,1)}, s32[]{:T(128)}, bf16[2,3072,768]{2,1,0:T(8,128)(2,1)}, ...), branch_computations={%region_1.0_spmd, %region_2.4_spmd} | conditional | flops 3628795392 | bytes 59778792 | solution.py:86
  300.9 4.3 gather_fusion.1
  305.3 5.0 %fusion = f32[128,768]{1,0:T(8,128)} fusion(bf16[2,768,3072]{2,1,0:T(8,128)(2,1)} %get-tuple-element.210, s32[]{:T(128)S(6)} %select_n.21, bf16[128,3072]{1,0:T(8,128)(2,1)} %gather_fusion.1, f32[128]{0:T(128)S(1)} %dynamic_slice.22), kind=kOutput, calls=%fused_computation.4 | convolution fusion | flops 605159424 | bytes 5898756 | tf_op jit(solution)/shard_map/while/body/eval_jaxpr/cond/branch_1_fun/dot_general | solution.py:35
  310.3 4.3 gather_fusion
  314.7 3.4 fusion.10
  318.1 4.0 fusion.4
  325.3 5.3 %fusion.18 = f32[128,3072]{1,0:T(8,128)} fusion(f32[128,3072]{1,0:T(8,128)S(1)} %fusion.4, bf16[2,3072,768]{2,1,0:T(8,128)(2,1)} %get-tuple-element.207, s32[]{:T(128)S(6)} %select_n.21, f32[128,768]{1,0:T(8,128)S(1)} %fusion.10, f32[128,768]{1,0:T(8,128)S(1)} %copy-done.2, f32[128,768]{1,0:T(8,128)S(1)} %fusion.6), kind=kOutput, calls=%fused_computation.22 | convolution fusion | flops 605356032 | bytes 9043972 | tf_op jit(solution)/shard_map/while/body/eval_jaxpr/cond/branch_1_fun/dot_general | solution.py:38
  330.6 7.0 %scatter_fusion.1 = f32[256,3072]{1,0:T(8,128)} fusion(f32[256,3072]{1,0:T(8,128)} %get-tuple-element.212, s32[128]{0:T(128)S(1)} %compare_select_fusion, f32[128,3072]{1,0:T(8,128)} %fusion.18), kind=kCustom, calls=%fused_computation.3 | custom fusion | flops 393216 | bytes 4719104 | tf_op jit(solution)/shard_map/while/body/eval_jaxpr/cond/branch_1_fun/scatter-add | solution.py:42
  337.6 4.4 fusion.21
  342.1 4.6 scatter_fusion
  348.0 47.3 %conditional.2 = ((f32[256,3072]{1,0:T(8,128)S(1)}, f32[256,3072]{1,0:T(8,128)})) conditional(s32[]{:T(128)} %convert_element_type.63, (f32[256,3072]{1,0:T(8,128)S(1)}, f32[256,3072]{1,0:T(8,128)}) %tuple.42, (s32[]{:T(128)}, s32[512]{0:T(512)}, bf16[256,3072]{1,0:T(8,128)(2,1)}, s32[]{:T(128)}, bf16[2,3072,768]{2,1,0:T(8,128)(2,1)}, ...), branch_computations={%region_1.0_spmd, %region_2.4_spmd} | conditional | flops 3628795392 | bytes 59778792 | solution.py:86
  349.4 4.3 gather_fusion.1
  353.8 5.0 %fusion = f32[128,768]{1,0:T(8,128)} fusion(bf16[2,768,3072]{2,1,0:T(8,128)(2,1)} %get-tuple-element.210, s32[]{:T(128)S(6)} %select_n.21, bf16[128,3072]{1,0:T(8,128)(2,1)} %gather_fusion.1, f32[128]{0:T(128)S(1)} %dynamic_slice.22), kind=kOutput, calls=%fused_computation.4 | convolution fusion | flops 605159424 | bytes 5898756 | tf_op jit(solution)/shard_map/while/body/eval_jaxpr/cond/branch_1_fun/dot_general | solution.py:35
  358.9 4.3 gather_fusion
  363.2 3.4 fusion.10
  366.6 4.0 fusion.4
  373.8 5.3 %fusion.18 = f32[128,3072]{1,0:T(8,128)} fusion(f32[128,3072]{1,0:T(8,128)S(1)} %fusion.4, bf16[2,3072,768]{2,1,0:T(8,128)(2,1)} %get-tuple-element.207, s32[]{:T(128)S(6)} %select_n.21, f32[128,768]{1,0:T(8,128)S(1)} %fusion.10, f32[128,768]{1,0:T(8,128)S(1)} %copy-done.2, f32[128,768]{1,0:T(8,128)S(1)} %fusion.6), kind=kOutput, calls=%fused_computation.22 | convolution fusion | flops 605356032 | bytes 9043972 | tf_op jit(solution)/shard_map/while/body/eval_jaxpr/cond/branch_1_fun/dot_general | solution.py:38
  379.1 7.0 %scatter_fusion.1 = f32[256,3072]{1,0:T(8,128)} fusion(f32[256,3072]{1,0:T(8,128)} %get-tuple-element.212, s32[128]{0:T(128)S(1)} %compare_select_fusion, f32[128,3072]{1,0:T(8,128)} %fusion.18), kind=kCustom, calls=%fused_computation.3 | custom fusion | flops 393216 | bytes 4719104 | tf_op jit(solution)/shard_map/while/body/eval_jaxpr/cond/branch_1_fun/scatter-add | solution.py:42
  386.2 4.4 fusion.21
  390.6 4.6 scatter_fusion
  403.5 36.2 %reduce-scatter.7.cloned.1.call-done = bf16[384,256]{1,0:T(8,128)(2,1)} async-done(((bf16[3072,256]{1,0:T(8,128)(2,1)}), bf16[384,256]{1,0:T(8,128)(2,1)}) %reduce-scatter.7.cloned.1.call-update) | async-done | bytes 196624
  441.4 40.0 %reduce-scatter.9.cloned.1.call-done = bf16[384,256]{1,0:T(8,128)(2,1)} async-done(((bf16[3072,256]{1,0:T(8,128)(2,1)}), bf16[384,256]{1,0:T(8,128)(2,1)}) %reduce-scatter.9.cloned.1.call-update) | async-done | bytes 196624
  (71 shorter events, 35.3 us)
Async XLA Ops:
  7.2 6.1 %copy-start.4 = (s32[512]{0:T(512)S(1)}, s32[512]{0:T(512)}, u32[]{:S(2)}) copy-start(s32[512]{0:T(512)} %param.18) | copy-start | bytes 6148
  7.2 66.6 %all-gather.8.cloned.1.call-start = ((), (), s32[]{:S(2)}) async-start(), calls=%async_computation.4 | async-start | bytes 9732096 | tf_op jit(solution)/shard_map/all_gather | solution.py:63
  9.5 126.7 %all-gather.4.cloned.1.call-start = ((), (), s32[]{:S(2)}) async-start(), calls=%async_computation.2 | async-start | bytes 9732096 | tf_op jit(solution)/shard_map/all_gather | solution.py:60
  11.4 187.3 %all-gather.6.cloned.1.call-start = ((), (), s32[]{:S(2)}) async-start(), calls=%async_computation.3 | async-start | bytes 9732096 | tf_op jit(solution)/shard_map/all_gather | solution.py:61
  13.2 426.4 %reduce-scatter.7.cloned.1.call-start = ((), (), s32[]{:S(2)}) async-start(), calls=%async_computation.5 | async-start | bytes 1769472
  97.5 103.6 %copy-start.5 = (s32[4]{0:T(128)S(1)}, s32[4]{0:T(128)}, u32[]{:S(2)}) copy-start(s32[4]{0:T(128)} %param.19) | copy-start | bytes 52
  217.6 3.4 copy-start.2
  221.0 4.1 copy-start.1
  228.2 5.3 %copy-start.3 = (f32[128,768]{1,0:T(8,128)}, f32[128,768]{1,0:T(8,128)S(1)}, u32[]{:S(2)}) copy-start(f32[128,768]{1,0:T(8,128)S(1)} %fusion.6) | copy-start | bytes 1179652 | tf_op jit(solution)/shard_map/while/body/eval_jaxpr/cond
  266.1 3.4 copy-start.2
  269.6 4.0 copy-start.1
  276.8 5.3 %copy-start.3 = (f32[128,768]{1,0:T(8,128)}, f32[128,768]{1,0:T(8,128)S(1)}, u32[]{:S(2)}) copy-start(f32[128,768]{1,0:T(8,128)S(1)} %fusion.6) | copy-start | bytes 1179652 | tf_op jit(solution)/shard_map/while/body/eval_jaxpr/cond
  314.7 3.4 copy-start.2
  318.1 4.0 copy-start.1
  325.3 5.3 %copy-start.3 = (f32[128,768]{1,0:T(8,128)}, f32[128,768]{1,0:T(8,128)S(1)}, u32[]{:S(2)}) copy-start(f32[128,768]{1,0:T(8,128)S(1)} %fusion.6) | copy-start | bytes 1179652 | tf_op jit(solution)/shard_map/while/body/eval_jaxpr/cond
  363.2 3.4 copy-start.2
  366.6 4.0 copy-start.1
  373.8 5.3 %copy-start.3 = (f32[128,768]{1,0:T(8,128)}, f32[128,768]{1,0:T(8,128)S(1)}, u32[]{:S(2)}) copy-start(f32[128,768]{1,0:T(8,128)S(1)} %fusion.6) | copy-start | bytes 1179652 | tf_op jit(solution)/shard_map/while/body/eval_jaxpr/cond
  396.6 2.8 copy-start
  399.4 82.0 %reduce-scatter.9.cloned.1.call-start = ((), (), s32[]{:S(2)}) async-start(), calls=%async_computation.6 | async-start | bytes 1769472
Sparse Core Ops, SparseCore 0:
  10.5 63.1 all-gather.7
  76.3 59.8 all-gather.3
  138.8 59.8 all-gather.5
  399.5 40.0 reduce-scatter.6
  442.1 39.2 reduce-scatter.8
where the time goes:
time: 492 us; the launch traced here: 490 us
  waiting for transfers between devices  238 us (48%)
  matrix products  101 us (21%)
  local copies, waits for them, and re-layouts  74.6 us (15%)
  other arithmetic  56.1 us (11%)
  between operations  13.8 us (3%)
  loops' own time  5.68 us (1%)
    unnamed x7, waiting for transfers between devices  76.3 us
    all_gather x1, waiting for transfers between devices, shards(): lax.all_gather(up_low, 'dp', axis=1, tiled=True)  62.5 us
    all_gather x1, waiting for transfers between devices, shards(): down_all = lax.all_gather(down_low, 'dp', axis=2, tiled=True)  60.4 us
    all_gather x1, waiting for transfers between devices, shards(): lax.all_gather(gate_low, 'dp', axis=1, tiled=True)  38.7 us
    scatter-add x4, other arithmetic, block_terms(): dx_total.at[token_rows].add(backward)  28.2 us
    while x1, local copies, waits for them, and re-layouts, shards(): totals = lax.fori_loop(0, block_count, visit_all, totals)  23.8 us
    dot_general x4, matrix products, block_terms(): lax.dot_general(d_pre, gate_mat, contract_last, preferred_element_type=jn...  21.2 us
    dot_general x4, matrix products, block_terms(): lax.dot_general(d_out, down_mat, contract_last, preferred_element_type=jn...  20.1 us
  transfers between devices with their start and end apart: 5, of which 5 were waited for; matrix products, arithmetic and copies ran while one was open for 7% of the time, Pallas kernels for 0%

commit v1 on v0

--- a/solution.py
+++ b/solution.py
@@ -60,7 +60,9 @@
         lax.all_gather(gate_low, "dp", axis=1, tiled=True),
         lax.all_gather(up_low, "dp", axis=1, tiled=True),
     )
-    down_all = lax.all_gather(down_low, "dp", axis=2, tiled=True)
+    down_all = jnp.concatenate(
+        lax.all_to_all(jnp.stack([down_low] * lax.axis_size("dp")), "dp", 0, 0), axis=2
+    )
 
     def visit_all(block_index, state):
         expert = block_expert[block_index]

time: 492 us -> 522 us (1.061)
  waiting for transfers between devices: 238 us -> 259 us
  starting transfers between devices: 0.21 us -> 7.97 us
    all_to_all x0 -> x1, waiting for transfers between devices: none -> 136 us  [shards(): lax.all_to_all(jnp.stack([down_low] * lax.axis_size('dp')), 'dp', 0, 0)]
    all_gather x1 -> x0, waiting for transfers between devices: 60.4 us -> none  [shards(): down_all = lax.all_gather(down_low, 'dp', axis=2, tiled=True)]
    all_gather x1, waiting for transfers between devices: 38.7 us -> 0.01 us  [shards(): lax.all_gather(gate_low, 'dp', axis=1, tiled=True)]
    all_gather x1, waiting for transfers between devices: 62.5 us -> 47.1 us  [shards(): lax.all_gather(up_low, 'dp', axis=1, tiled=True)]
    while x1, local copies, waits for them, and re-layouts: 23.8 us -> 12.7 us  [shards(): totals = lax.fori_loop(0, block_count, visit_all, totals)]
    all_to_all x0 -> x1, local copies, waits for them, and re-layouts: none -> 8.13 us  [shards(): lax.all_to_all(jnp.stack([down_low] * lax.axis_size('dp')), 'dp', 0, 0)]
    all_to_all x0 -> x1, starting transfers between devices: none -> 7.8 us  [shards(): lax.all_to_all(jnp.stack([down_low] * lax.axis_size('dp')), 'dp', 0, 0)]
    unnamed x11 -> x10, local copies, waits for them, and re-layouts: 11.1 us -> 8.82 us
  transfers between devices with their start and end apart: 5 -> 5, of which waited for: 5 -> 4; matrix products, arithmetic and copies ran while one was open for 7% -> 7% of each run, Pallas kernels for 0% -> 0%
where the time goes in v1:
time: 522 us; the launch traced here: 520 us
  waiting for transfers between devices  259 us (50%)
  matrix products  101 us (19%)
  local copies, waits for them, and re-layouts  74.3 us (14%)
  other arithmetic  57.2 us (11%)
  between operations  13.8 us (3%)
  starting transfers between devices  7.97 us (2%)
  loops' own time  5.68 us (1%)
    all_to_all x1, waiting for transfers between devices, shards(): lax.all_to_all(jnp.stack([down_low] * lax.axis_size('dp')), 'dp', 0, 0)  136 us
    unnamed x6, waiting for transfers between devices  76.3 us
    all_gather x1, waiting for transfers between devices, shards(): lax.all_gather(up_low, 'dp', axis=1, tiled=True)  47.1 us
    scatter-add x4, other arithmetic, block_terms(): dx_total.at[token_rows].add(backward)  28.2 us
    dot_general x4, matrix products, block_terms(): lax.dot_general(d_pre, gate_mat, contract_last, preferred_element_type=jn...  21.2 us
    dot_general x4, matrix products, block_terms(): lax.dot_general(d_out, down_mat, contract_last, preferred_element_type=jn...  20.1 us
    scatter-add x4, other arithmetic, block_terms(): y_total.at[token_rows].add(produced)  18.5 us
    dot_general x4, matrix products, block_terms(): jnp.dot(hidden, down_mat, preferred_element_type=jnp.float32) * gate_scale  17.8 us
  transfers between devices with their start and end apart: 5, of which 4 were waited for; matrix products, arithmetic and copies ran while one was open for 7% of the time, Pallas kernels for 0%

profile of v1, /device:TPU:2, one launch (start us, length us, event | category | flops | bytes accessed | tf_op | source)
XLA Modules:
  0.0 519.6 jit_solution(337826109244909726)
XLA Ops:
  12.0 4.8 stack.2
  16.9 7.8 %all-to-all-start = ((bf16[32,2,768,96]{2,3,1,0:T(8,128)(2,1)}), bf16[32,2,768,96]{2,3,1,0:T(8,128)(2,1)}, u32[]{:S(2)}, u32[]{:S(2)}) async-start(bf16[32,2,768,96]{2,3,1,0:T(8,128)(2,1)} %stack.2), calls=%async_computation | async-start | bytes 18874368 | tf_op jit(solution)/shard_map/all_to_all | solution.py:64
  24.7 135.8 %all-to-all-done = bf16[32,2,768,96]{2,3,1,0:T(8,128)(2,1)} async-done(((bf16[32,2,768,96]{2,3,1,0:T(8,128)(2,1)}), bf16[32,2,768,96]{2,3,1,0:T(8,128)(2,1)}, u32[]{:S(2)}, u32[]{:S(2)}) %all-to-all-start) | async-done | bytes 9437216 | tf_op jit(solution)/shard_map/all_to_all | solution.py:64
  160.6 8.1 %copy.12 = bf16[32,2,768,96]{2,3,0,1:T(8,128)(2,1)} copy(bf16[32,2,768,96]{2,3,1,0:T(8,128)(2,1)} %all-to-all-done) | data formatting | bytes 18874368 | tf_op jit(solution)/shard_map/all_to_all | solution.py:64
  168.7 12.7 %copy.13 = bf16[2,768,3072]{2,1,0:T(8,128)(2,1)} copy(bf16[2,768,3072]{1,2,0:T(8,128)(2,1)} %bitcast.31) | data formatting | bytes 18874368 | tf_op jit(solution)/shard_map/while | solution.py:90
  181.4 47.1 %all-gather.5.cloned.1.call-done = bf16[2,3072,768]{2,1,0:T(8,128)(2,1)} async-done(((bf16[2,96,768]{2,1,0:T(8,128)(2,1)}), bf16[2,3072,768]{2,1,0:T(8,128)(2,1)}) %all-gather.5.cloned.1.call-update) | async-done | bytes 9437200 | tf_op jit(solution)/shard_map/all_gather | solution.py:61
  231.0 194.2 %while.15 = (s32[]{:T(128)}, f32[256,3072]{1,0:T(8,128)S(1)}, f32[256,3072]{1,0:T(8,128)}, s32[4]{0:T(128)S(1)}, s32[512]{0:T(512)}, /*index=5*/bf16[256,3072]{1...) while((s32[]{:T(128)}, f32[256,3072]{1,0:T(8,128)S(1)}, ...), condition=%wide.region_5.6_spmd, body=%wide.region_0.5_spmd.sunk | while | flops 3628795392 | bytes 59779048 | solution.py:90
  232.2 47.3 %conditional.2 = ((f32[256,3072]{1,0:T(8,128)S(1)}, f32[256,3072]{1,0:T(8,128)})) conditional(s32[]{:T(128)} %convert_element_type.62, (f32[256,3072]{1,0:T(8,128)S(1)}, f32[256,3072]{1,0:T(8,128)}) %tuple.43, (s32[]{:T(128)}, s32[512]{0:T(512)}, bf16[256,3072]{1,0:T(8,128)(2,1)}, s32[]{:T(128)}, bf16[2,3072,768]{2,1,0:T(8,128)(2,1)}, ...), branch_computations={%region_1.0_spmd, %region_2.4_spmd} | conditional | flops 3628795392 | bytes 59778792 | solution.py:88
  233.7 4.3 gather_fusion.1
  238.1 5.0 fusion
  243.1 4.3 gather_fusion
  250.9 4.0 fusion.4
  258.1 5.3 %fusion.18 = f32[128,3072]{1,0:T(8,128)} fusion(f32[128,3072]{1,0:T(8,128)S(1)} %fusion.4, bf16[2,3072,768]{2,1,0:T(8,128)(2,1)} %get-tuple-element.207, s32[]{:T(128)S(6)} %select_n.21, f32[128,768]{1,0:T(8,128)S(1)} %fusion.10, f32[128,768]{1,0:T(8,128)S(1)} %copy-done.2, f32[128,768]{1,0:T(8,128)S(1)} %fusion.6), kind=kOutput, calls=%fused_computation.22 | convolution fusion | flops 605356032 | bytes 9043972 | tf_op jit(solution)/shard_map/while/body/eval_jaxpr/cond/branch_1_fun/dot_general | solution.py:38
  263.4 7.0 %scatter_fusion.1 = f32[256,3072]{1,0:T(8,128)} fusion(f32[256,3072]{1,0:T(8,128)} %get-tuple-element.212, s32[128]{0:T(128)S(1)} %compare_select_fusion, f32[128,3072]{1,0:T(8,128)} %fusion.18), kind=kCustom, calls=%fused_computation.3 | custom fusion | flops 393216 | bytes 4719104 | tf_op jit(solution)/shard_map/while/body/eval_jaxpr/cond/branch_1_fun/scatter-add | solution.py:42
  270.4 4.4 fusion.21
  274.9 4.6 scatter_fusion
  280.8 47.3 %conditional.2 = ((f32[256,3072]{1,0:T(8,128)S(1)}, f32[256,3072]{1,0:T(8,128)})) conditional(s32[]{:T(128)} %convert_element_type.62, (f32[256,3072]{1,0:T(8,128)S(1)}, f32[256,3072]{1,0:T(8,128)}) %tuple.43, (s32[]{:T(128)}, s32[512]{0:T(512)}, bf16[256,3072]{1,0:T(8,128)(2,1)}, s32[]{:T(128)}, bf16[2,3072,768]{2,1,0:T(8,128)(2,1)}, ...), branch_computations={%region_1.0_spmd, %region_2.4_spmd} | conditional | flops 3628795392 | bytes 59778792 | solution.py:88
  282.2 4.3 gather_fusion.1
  286.6 5.0 fusion
  291.7 4.3 gather_fusion
  296.0 3.4 fusion.10
  299.4 4.0 fusion.4
  306.6 5.3 %fusion.18 = f32[128,3072]{1,0:T(8,128)} fusion(f32[128,3072]{1,0:T(8,128)S(1)} %fusion.4, bf16[2,3072,768]{2,1,0:T(8,128)(2,1)} %get-tuple-element.207, s32[]{:T(128)S(6)} %select_n.21, f32[128,768]{1,0:T(8,128)S(1)} %fusion.10, f32[128,768]{1,0:T(8,128)S(1)} %copy-done.2, f32[128,768]{1,0:T(8,128)S(1)} %fusion.6), kind=kOutput, calls=%fused_computation.22 | convolution fusion | flops 605356032 | bytes 9043972 | tf_op jit(solution)/shard_map/while/body/eval_jaxpr/cond/branch_1_fun/dot_general | solution.py:38
  311.9 7.0 %scatter_fusion.1 = f32[256,3072]{1,0:T(8,128)} fusion(f32[256,3072]{1,0:T(8,128)} %get-tuple-element.212, s32[128]{0:T(128)S(1)} %compare_select_fusion, f32[128,3072]{1,0:T(8,128)} %fusion.18), kind=kCustom, calls=%fused_computation.3 | custom fusion | flops 393216 | bytes 4719104 | tf_op jit(solution)/shard_map/while/body/eval_jaxpr/cond/branch_1_fun/scatter-add | solution.py:42
  319.0 4.4 fusion.21
  323.4 4.6 scatter_fusion
  329.3 47.3 %conditional.2 = ((f32[256,3072]{1,0:T(8,128)S(1)}, f32[256,3072]{1,0:T(8,128)})) conditional(s32[]{:T(128)} %convert_element_type.62, (f32[256,3072]{1,0:T(8,128)S(1)}, f32[256,3072]{1,0:T(8,128)}) %tuple.43, (s32[]{:T(128)}, s32[512]{0:T(512)}, bf16[256,3072]{1,0:T(8,128)(2,1)}, s32[]{:T(128)}, bf16[2,3072,768]{2,1,0:T(8,128)(2,1)}, ...), branch_computations={%region_1.0_spmd, %region_2.4_spmd} | conditional | flops 3628795392 | bytes 59778792 | solution.py:88
  330.8 4.3 gather_fusion.1
  335.2 5.0 fusion
  340.2 4.3 gather_fusion
  344.6 3.4 fusion.10
  348.0 4.0 fusion.4
  355.2 5.3 %fusion.18 = f32[128,3072]{1,0:T(8,128)} fusion(f32[128,3072]{1,0:T(8,128)S(1)} %fusion.4, bf16[2,3072,768]{2,1,0:T(8,128)(2,1)} %get-tuple-element.207, s32[]{:T(128)S(6)} %select_n.21, f32[128,768]{1,0:T(8,128)S(1)} %fusion.10, f32[128,768]{1,0:T(8,128)S(1)} %copy-done.2, f32[128,768]{1,0:T(8,128)S(1)} %fusion.6), kind=kOutput, calls=%fused_computation.22 | convolution fusion | flops 605356032 | bytes 9043972 | tf_op jit(solution)/shard_map/while/body/eval_jaxpr/cond/branch_1_fun/dot_general | solution.py:38
  360.5 7.0 %scatter_fusion.1 = f32[256,3072]{1,0:T(8,128)} fusion(f32[256,3072]{1,0:T(8,128)} %get-tuple-element.212, s32[128]{0:T(128)S(1)} %compare_select_fusion, f32[128,3072]{1,0:T(8,128)} %fusion.18), kind=kCustom, calls=%fused_computation.3 | custom fusion | flops 393216 | bytes 4719104 | tf_op jit(solution)/shard_map/while/body/eval_jaxpr/cond/branch_1_fun/scatter-add | solution.py:42
  367.6 4.4 fusion.21
  372.0 4.6 scatter_fusion
  377.9 47.3 %conditional.2 = ((f32[256,3072]{1,0:T(8,128)S(1)}, f32[256,3072]{1,0:T(8,128)})) conditional(s32[]{:T(128)} %convert_element_type.62, (f32[256,3072]{1,0:T(8,128)S(1)}, f32[256,3072]{1,0:T(8,128)}) %tuple.43, (s32[]{:T(128)}, s32[512]{0:T(512)}, bf16[256,3072]{1,0:T(8,128)(2,1)}, s32[]{:T(128)}, bf16[2,3072,768]{2,1,0:T(8,128)(2,1)}, ...), branch_computations={%region_1.0_spmd, %region_2.4_spmd} | conditional | flops 3628795392 | bytes 59778792 | solution.py:88
  379.4 4.3 gather_fusion.1
  383.8 5.0 fusion
  388.8 4.3 gather_fusion
  393.1 3.4 fusion.10
  396.6 4.0 fusion.4
  403.8 5.3 %fusion.18 = f32[128,3072]{1,0:T(8,128)} fusion(f32[128,3072]{1,0:T(8,128)S(1)} %fusion.4, bf16[2,3072,768]{2,1,0:T(8,128)(2,1)} %get-tuple-element.207, s32[]{:T(128)S(6)} %select_n.21, f32[128,768]{1,0:T(8,128)S(1)} %fusion.10, f32[128,768]{1,0:T(8,128)S(1)} %copy-done.2, f32[128,768]{1,0:T(8,128)S(1)} %fusion.6), kind=kOutput, calls=%fused_computation.22 | convolution fusion | flops 605356032 | bytes 9043972 | tf_op jit(solution)/shard_map/while/body/eval_jaxpr/cond/branch_1_fun/dot_general | solution.py:38
  409.1 7.0 %scatter_fusion.1 = f32[256,3072]{1,0:T(8,128)} fusion(f32[256,3072]{1,0:T(8,128)} %get-tuple-element.212, s32[128]{0:T(128)S(1)} %compare_select_fusion, f32[128,3072]{1,0:T(8,128)} %fusion.18), kind=kCustom, calls=%fused_computation.3 | custom fusion | flops 393216 | bytes 4719104 | tf_op jit(solution)/shard_map/while/body/eval_jaxpr/cond/branch_1_fun/scatter-add | solution.py:42
  416.1 4.4 fusion.21
  420.6 4.6 scatter_fusion
  433.4 36.2 %reduce-scatter.7.cloned.1.call-done = bf16[384,256]{1,0:T(8,128)(2,1)} async-done(((bf16[3072,256]{1,0:T(8,128)(2,1)}), bf16[384,256]{1,0:T(8,128)(2,1)}) %reduce-scatter.7.cloned.1.call-update) | async-done | bytes 196624
  471.4 40.0 %reduce-scatter.9.cloned.1.call-done = bf16[384,256]{1,0:T(8,128)(2,1)} async-done(((bf16[3072,256]{1,0:T(8,128)(2,1)}), bf16[384,256]{1,0:T(8,128)(2,1)}) %reduce-scatter.9.cloned.1.call-update) | async-done | bytes 196624
  (72 shorter events, 40.6 us)
Async XLA Ops:
  7.2 174.2 %all-gather.3.cloned.1.call-start = ((), (), s32[]{:S(2)}) async-start(), calls=%async_computation.3 | async-start | bytes 9732096 | tf_op jit(solution)/shard_map/all_gather | solution.py:60
  9.1 219.5 %all-gather.5.cloned.1.call-start = ((), (), s32[]{:S(2)}) async-start(), calls=%async_computation.4 | async-start | bytes 9732096 | tf_op jit(solution)/shard_map/all_gather | solution.py:61
  16.9 7.9 %copy-start.4 = (s32[512]{0:T(512)S(1)}, s32[512]{0:T(512)}, u32[]{:S(2)}) copy-start(s32[512]{0:T(512)} %param.18) | copy-start | bytes 6148
  16.9 143.7 %all-to-all-start = ((bf16[32,2,768,96]{2,3,1,0:T(8,128)(2,1)}), bf16[32,2,768,96]{2,3,1,0:T(8,128)(2,1)}, u32[]{:S(2)}, u32[]{:S(2)}) async-start(bf16[32,2,768,96]{2,3,1,0:T(8,128)(2,1)} %stack.2), calls=%async_computation | async-start | bytes 18874368 | tf_op jit(solution)/shard_map/all_to_all | solution.py:64
  24.7 444.9 %reduce-scatter.7.cloned.1.call-start = ((), (), s32[]{:S(2)}) async-start(), calls=%async_computation.5 | async-start | bytes 1769472
  181.4 49.6 %copy-start.5 = (s32[4]{0:T(128)S(1)}, s32[4]{0:T(128)}, u32[]{:S(2)}) copy-start(s32[4]{0:T(128)} %param.19) | copy-start | bytes 52
  247.4 3.4 copy-start.2
  250.9 4.1 copy-start.1
  258.1 5.3 %copy-start.3 = (f32[128,768]{1,0:T(8,128)}, f32[128,768]{1,0:T(8,128)S(1)}, u32[]{:S(2)}) copy-start(f32[128,768]{1,0:T(8,128)S(1)} %fusion.6) | copy-start | bytes 1179652 | tf_op jit(solution)/shard_map/while/body/eval_jaxpr/cond
  296.0 3.4 copy-start.2
  299.4 4.1 copy-start.1
  306.6 5.3 %copy-start.3 = (f32[128,768]{1,0:T(8,128)}, f32[128,768]{1,0:T(8,128)S(1)}, u32[]{:S(2)}) copy-start(f32[128,768]{1,0:T(8,128)S(1)} %fusion.6) | copy-start | bytes 1179652 | tf_op jit(solution)/shard_map/while/body/eval_jaxpr/cond
  344.6 3.4 copy-start.2
  348.0 4.1 copy-start.1
  355.2 5.3 %copy-start.3 = (f32[128,768]{1,0:T(8,128)}, f32[128,768]{1,0:T(8,128)S(1)}, u32[]{:S(2)}) copy-start(f32[128,768]{1,0:T(8,128)S(1)} %fusion.6) | copy-start | bytes 1179652 | tf_op jit(solution)/shard_map/while/body/eval_jaxpr/cond
  393.1 3.4 copy-start.2
  396.6 4.1 copy-start.1
  403.8 5.3 %copy-start.3 = (f32[128,768]{1,0:T(8,128)}, f32[128,768]{1,0:T(8,128)S(1)}, u32[]{:S(2)}) copy-start(f32[128,768]{1,0:T(8,128)S(1)} %fusion.6) | copy-start | bytes 1179652 | tf_op jit(solution)/shard_map/while/body/eval_jaxpr/cond
  426.6 2.8 copy-start
  429.4 82.0 %reduce-scatter.9.cloned.1.call-start = ((), (), s32[]{:S(2)}) async-start(), calls=%async_computation.6 | async-start | bytes 1769472
Sparse Core Ops, SparseCore 0:
  10.6 150.3 all-gather.2
  163.6 64.9 all-gather.4
  429.5 40.0 reduce-scatter.6
  472.0 39.3 reduce-scatter.8
